TPU v7x, 256 devices: a whole 4x4x8 slice. The times are simulated.
256 devices in a mesh: fsdp: 32 (over x_hi, z, core), ctx: 8 (over x_lo, y).
Axes of the slice: x: 4 (x_hi: 2, x_lo: 2; x = x_hi * 2 + x_lo), y: 4, z: 8, core: 2. Of those that a mesh axis runs over, the one named last changes fastest.
Arguments:
- hidden: bfloat16 [2048, 8192], P('ctx', 'fsdp'), may hold values from -6 to 6
- gain: bfloat16 [8192], replicated, may hold values from 0.25 to 1.75
- embed: bfloat16 [512, 8192], P(None, 'fsdp'), may hold values from -6 to 6
- qkv_weight: bfloat16 [8192, 12288], P('fsdp'), may hold values from -0.07164475 to 0.07164475
- out_weight: bfloat16 [4096, 8192], P('fsdp'), may hold values from -1 to 1
- ref_ids: int32 [2048], P('ctx'), may hold values from 0 to 511
- var_pos: int32 [128], P('ctx'), may hold values from 0 to 2047, as said below
- var_base: int32 [128], P('ctx'), may hold values from 0 to 511
Outputs:
- mixed: bfloat16 [2, 2048, 8192], P(None, 'ctx', 'fsdp')
Inputs may be any that keep to these rules, and one draw needn't show every extreme that they name: Each block of 256 consecutive positions holds exactly 16 distinct variant positions, and they are listed among that block's 16 entries of var_pos.
All inputs are finite; a program needn't handle non-finite values.
Results may differ from a plain program's by a relative error of at most 0.025.
Values may be sent and summed in bfloat16 or wider, within the bound.
No kernel may reach another device: no remote copies, remote signals or barrier semaphores. Data moves between devices by JAX's collectives and lax.ppermute only.
A program may use at most 128 MiB of HBM per device.

v0:
```python
import jax
import jax.numpy as jnp
from jax import lax
from jax.sharding import PartitionSpec as P

epsilon = 1e-05
rope_base = 10000.0


def from_behind(block, axis, distance):
    devices = range(lax.axis_size(axis))
    route = [(i - distance, i) for i in devices if i - distance in devices]
    return lax.ppermute(block, axis, route)


def rotate(values, positions):
    half = values.shape[-1] // 2
    exponent = jnp.arange(half).astype(jnp.float32) * (-2.0 / values.shape[-1])
    inv_freq = jnp.power(jnp.float32(rope_base), exponent)
    angle = positions.astype(jnp.float32)[:, None] * inv_freq[None, :]
    cosine = jnp.cos(angle)
    sine = jnp.sin(angle)
    first = values[..., :half]
    second = values[..., half:]
    return jnp.concatenate(
        [first * cosine - second * sine, second * cosine + first * sine], axis=-1
    )


def shards(hidden, gain, embed, qkv_weight, out_weight, ref_ids, var_pos, var_base):
    tok_rows, width_part = hidden.shape
    head_size = out_weight.shape[0]
    full_width = out_weight.shape[1]
    vocab_size = embed.shape[0]
    my_block = lax.axis_index("ctx")
    cycle_len = lax.axis_size("ctx")
    local_pos = var_pos - my_block * tok_rows
    var_spots = local_pos[:, None] == jnp.arange(tok_rows)[None, :]
    placer = var_spots.T.astype(jnp.bfloat16)
    changed = jnp.any(var_spots, axis=0)
    ref_at = jnp.sum(jnp.where(var_spots, ref_ids[None, :], 0), axis=1)
    vocab_line = jnp.arange(vocab_size)[None, :]
    onehot_diff = (vocab_line == var_base[:, None]).astype(jnp.bfloat16) - (
        vocab_line == ref_at[:, None]
    ).astype(jnp.bfloat16)
    change = jnp.dot(onehot_diff, embed, preferred_element_type=jnp.float32)
    picked_rows = jnp.dot(
        var_spots.astype(jnp.bfloat16), hidden, preferred_element_type=jnp.float32
    )
    var_rows = (picked_rows + change).astype(jnp.bfloat16)
    placed_rows = jnp.dot(placer, var_rows, preferred_element_type=jnp.float32).astype(jnp.bfloat16)
    variant = jnp.where(changed[:, None], placed_rows, hidden)
    head_w = lax.all_to_all(qkv_weight, "fsdp", split_axis=1, concat_axis=0, tiled=True)
    block_pos = my_block * tok_rows + jnp.arange(tok_rows)

    def finish(proj_rows, positions):
        query_part = rotate(proj_rows[:, :head_size], positions)
        key_part = rotate(proj_rows[:, head_size : 2 * head_size], positions)
        return jnp.concatenate(
            [query_part, key_part, proj_rows[:, 2 * head_size :]], axis=1
        ).astype(jnp.bfloat16)

    dense_rows = jnp.concatenate([hidden, variant], axis=0)
    gain_part = gain.astype(jnp.float32)
    widened = lax.all_gather(dense_rows, "fsdp", axis=1, tiled=True).astype(jnp.float32)
    scaled = (widened * gain_part[None, :]).astype(jnp.bfloat16)
    running = jnp.dot(scaled, head_w, preferred_element_type=jnp.float32)
    running, squares = (running, jnp.sum(widened * widened, axis=1))
    inv_rms = lax.rsqrt(squares / full_width + epsilon)
    proj_all = running * inv_rms[:, None]
    ref_qkv = finish(proj_all[:tok_rows], block_pos)
    var_qkv = finish(proj_all[tok_rows:], block_pos)
    both_qkv = jnp.stack([ref_qkv, var_qkv])
    queries = both_qkv[:, :, :head_size]
    kv_blocks = jnp.stack(
        [both_qkv[:, :, head_size : 2 * head_size], both_qkv[:, :, 2 * head_size :]]
    )
    score_scale = 1.0 / head_size**0.5
    carried = (
        jnp.full((2, tok_rows), -jnp.inf, jnp.float32),
        jnp.zeros((2, tok_rows), jnp.float32),
        jnp.zeros((2, tok_rows, head_size), jnp.float32),
    )
    blocks_now = kv_blocks
    for rotation in range(cycle_len):
        source = my_block - rotation
        attend_top, attend_denom, attend_running = carried
        key_pos = source * tok_rows + jnp.arange(tok_rows)
        visible = (block_pos[:, None] >= key_pos[None, :]) & (source >= 0)
        score = (
            jnp.einsum("sqd,skd->sqk", queries, blocks_now[0], preferred_element_type=jnp.float32)
            * score_scale
        )
        score = jnp.where(visible[None], score, -jnp.inf)
        new_top = jnp.maximum(attend_top, jnp.max(score, axis=-1))
        safe_top = jnp.where(jnp.isfinite(new_top), new_top, 0.0)
        probs = jnp.exp(score - safe_top[..., None])
        factor = jnp.exp(attend_top - safe_top)
        attend_denom = attend_denom * factor + jnp.sum(probs, axis=-1)
        attend_running = attend_running * factor[..., None] + jnp.einsum(
            "sqk,skd->sqd",
            probs.astype(jnp.bfloat16),
            blocks_now[1],
            preferred_element_type=jnp.float32,
        )
        carried = (new_top, attend_denom, attend_running)
        if rotation + 1 < cycle_len:
            blocks_now = from_behind(blocks_now, "ctx", 1)
    top, denom, running = carried
    attn_flat = (running / denom[..., None]).astype(jnp.bfloat16).reshape(2 * tok_rows, head_size)
    branch = lax.psum_scatter(
        lax.dot_general(
            out_weight, attn_flat, (((0,), (1,)), ((), ())), preferred_element_type=jnp.float32
        ).astype(jnp.bfloat16),
        "fsdp",
        scatter_dimension=0,
        tiled=True,
    ).astype(jnp.float32)
    branch = branch.T.reshape(2, tok_rows, width_part)
    seqs = jnp.stack([hidden, variant]).astype(jnp.float32)
    return (seqs + branch).astype(jnp.bfloat16)


def solution(mesh):
    in_specs = (
        P("ctx", "fsdp"),
        P(),
        P(None, "fsdp"),
        P("fsdp", None),
        P("fsdp", None),
        P("ctx"),
        P("ctx"),
        P("ctx"),
    )
    out_specs = P(None, "ctx", "fsdp")
    return jax.shard_map(shards, mesh=mesh, in_specs=in_specs, out_specs=out_specs, check_vma=False)
```

profile of v0, /device:TPU:8, one launch (start us, length us, event | category | flops | bytes accessed | tf_op | source)
XLA Modules:
  0.0 472.9 jit_solution(10370490574901621818)
XLA Ops:
  10.8 1.6 pad_maximum_fusion
  12.5 8.6 %copy.107 = bf16[256,12288]{0,1:T(8,128)(2,1)} copy(bf16[256,12288]{1,0:T(8,128)(2,1)} %param.11) | data formatting | bytes 12582912 | tf_op args[3]
  21.0 11.6 %all-to-all-start = ((bf16[256,32,384]{0,2,1:T(8,128)(2,1)}), bf16[256,32,384]{0,2,1:T(8,128)(2,1)}, u32[]{:S(2)}, u32[]{:S(2)}) async-start(bf16[256,32,384]{0,2,1:T(8,128)(2,1)} %bitcast.108), calls=%async_computation | async-start | bytes 12582912 | tf_op jit(solution)/shard_map/all_to_all | solution.py:53
  32.7 161.2 %all-to-all-done = bf16[256,32,384]{0,2,1:T(8,128)(2,1)} async-done(((bf16[256,32,384]{0,2,1:T(8,128)(2,1)}), bf16[256,32,384]{0,2,1:T(8,128)(2,1)}, u32[]{:S(2)}, u32[]{:S(2)}) %all-to-all-start) | async-done | bytes 6291488 | tf_op jit(solution)/shard_map/all_to_all | solution.py:53
  193.9 8.6 %copy.108 = bf16[32,256,384]{2,1,0:T(8,128)(2,1)} copy(bf16[32,256,384]{1,2,0:T(8,128)(2,1)} %bitcast.3) | data formatting | bytes 12582912 | tf_op jit(solution)/shard_map/all_to_all | solution.py:53
  202.5 5.2 %all-gather.2.cloned.1.call-done = bf16[512,8192]{1,0:T(8,128)(2,1)} async-done(((bf16[512,256]{1,0:T(8,128)(2,1)}), bf16[512,8192]{1,0:T(8,128)(2,1)}) %all-gather.2.cloned.1.call-update) | async-done | bytes 8388624 | tf_op jit(solution)/shard_map/all_gather | solution.py:65
  207.8 5.3 %fusion.1 = f32[512]{0:T(512)S(1)} fusion(bf16[512,8192]{1,0:T(8,128)(2,1)} %all-gather.2.cloned.1.call-done), kind=kLoop, calls=%fused_computation.3 | loop fusion | flops 12582400 | bytes 8390656 | tf_op jit(solution)/shard_map/reduce_sum | solution.py:68
  213.6 7.1 %fusion.115 = (bf16[512,384]{0,1:T(8,128)(2,1)}, f32[512,384]{0,1:T(8,128)S(1)}) fusion(f32[512]{0:T(512)S(1)} %add_rsqrt_fusion, bf16[8192,384]{1,0:T(8,128)(2,1)} %bitcast.109, bf16[512,8192]{1,0:T(8,128)(2,1)S(1)} %copy-done.1, f32[8192]{0:T(1024)S(1)} %convert_element_type.105), kind=kOutput, calls=%fused_computation.200 | convolution fusion | flops 3234201600 | bytes 15894528 | tf_op jit(solution)/shard_map/dot_general | solution.py:67
  223.5 3.4 collective-permute-start
  226.9 7.0 %collective-permute-done = bf16[2,2,256,128]{2,3,1,0:T(8,128)(2,1)S(1)} collective-permute-done((bf16[2,2,256,128]{2,3,1,0:T(8,128)(2,1)S(1)}, bf16[2,2,256,128]{2,3,1,0:T(8,128)(2,1)S(1)}, u32[]{:S(2)}, u32[]{:S(2)}) %collective-permute-start) | collective-permute-done | bytes 262176 | tf_op jit(solution)/shard_map/ppermute | solution.py:13
  233.9 3.4 collective-permute-start.1
  237.3 6.1 %collective-permute-done.1 = bf16[2,2,256,128]{2,3,1,0:T(8,128)(2,1)S(1)} collective-permute-done((bf16[2,2,256,128]{2,3,1,0:T(8,128)(2,1)S(1)}, bf16[2,2,256,128]{2,3,1,0:T(8,128)(2,1)S(1)}, u32[]{:S(2)}, u32[]{:S(2)}) %collective-permute-start.1) | collective-permute-done | bytes 262176 | tf_op jit(solution)/shard_map/ppermute | solution.py:13
  243.5 3.4 collective-permute-start.2
  246.9 5.2 %collective-permute-done.2 = bf16[2,2,256,128]{2,3,1,0:T(8,128)(2,1)S(1)} collective-permute-done((bf16[2,2,256,128]{2,3,1,0:T(8,128)(2,1)S(1)}, bf16[2,2,256,128]{2,3,1,0:T(8,128)(2,1)S(1)}, u32[]{:S(2)}, u32[]{:S(2)}) %collective-permute-start.2) | collective-permute-done | bytes 262176 | tf_op jit(solution)/shard_map/ppermute | solution.py:13
  252.1 3.4 collective-permute-start.3
  256.3 4.0 collective-permute-done.3
  260.3 3.8 collective-permute-start.4
  264.7 4.0 collective-permute-done.4
  268.7 5.8 %collective-permute-start.5 = (bf16[2,2,256,128]{2,3,1,0:T(8,128)(2,1)S(1)}, bf16[2,2,256,128]{2,3,1,0:T(8,128)(2,1)S(1)}, u32[]{:S(2)}, u32[]{:S(2)}) collective-permute-start(bf16[2,2,256,128]{2,3,1,0:T(8,128)(2,1)S(1)} %collective-permute-done.4), channel_id=1, source_target_pairs={{0,1},{1,2},{2,3},{3,4},{4,5},{5,6},{6,7},{8,9},{9,10},{10,11},{11... | collective-permute-start | bytes 786440 | tf_op jit(solution)/shard_map/ppermute | solution.py:13
  275.1 3.3 collective-permute-done.5
  278.4 6.7 %collective-permute-start.6 = (bf16[2,2,256,128]{2,3,1,0:T(8,128)(2,1)S(1)}, bf16[2,2,256,128]{2,3,1,0:T(8,128)(2,1)S(1)}, u32[]{:S(2)}, u32[]{:S(2)}) collective-permute-start(bf16[2,2,256,128]{2,3,1,0:T(8,128)(2,1)S(1)} %collective-permute-done.5), channel_id=1, source_target_pairs={{0,1},{1,2},{2,3},{3,4},{4,5},{5,6},{6,7},{8,9},{9,10},{10,11},{11... | collective-permute-start | bytes 786440 | tf_op jit(solution)/shard_map/ppermute | solution.py:13
  285.6 3.1 collective-permute-done.6
  293.3 5.6 %fusion.2 = bf16[8192,512]{0,1:T(8,128)(2,1)} fusion(bf16[512,128]{1,0:T(8,128)(2,1)S(1)} %bitcast.113, bf16[128,8192]{1,0:T(8,128)(2,1)S(1)} %copy-done), kind=kOutput, calls=%fused_computation.5 | convolution fusion | flops 1077936128 | bytes 10616832 | tf_op jit(solution)/shard_map/dot_general | solution.py:112
  298.9 165.4 %reduce-scatter.2.cloned.1.call-done = bf16[256,512]{0,1:T(8,128)(2,1)} async-done(((bf16[8192,512]{0,1:T(8,128)(2,1)}), bf16[256,512]{0,1:T(8,128)(2,1)}) %reduce-scatter.2.cloned.1.call-update) | async-done | bytes 262160 | tf_op jit(solution)/shard_map/reduce_scatter | solution.py:111
  (71 shorter events, 16.5 us)
Async XLA Ops:
  6.5 286.8 %copy-start = (bf16[128,8192]{1,0:T(8,128)(2,1)S(1)}, bf16[128,8192]{1,0:T(8,128)(2,1)}, u32[]{:S(2)}) copy-start(bf16[128,8192]{1,0:T(8,128)(2,1)} %param.12) | copy-start | bytes 6291460
  6.5 201.2 %all-gather.2.cloned.1.call-start = ((), (), s32[]{:S(2)}) async-start(), calls=%async_computation.2 | async-start | bytes 8650752 | tf_op jit(solution)/shard_map/all_gather | solution.py:65
  21.0 11.6 %copy-start.4 = (bf16[8192]{0:T(1024)(128)(2,1)S(1)}, bf16[8192]{0:T(1024)(128)(2,1)}, u32[]{:S(2)}) copy-start(bf16[8192]{0:T(1024)(128)(2,1)} %param.9) | copy-start | bytes 49156
  21.0 172.9 %all-to-all-start = ((bf16[256,32,384]{0,2,1:T(8,128)(2,1)}), bf16[256,32,384]{0,2,1:T(8,128)(2,1)}, u32[]{:S(2)}, u32[]{:S(2)}) async-start(bf16[256,32,384]{0,2,1:T(8,128)(2,1)} %bitcast.108), calls=%async_computation | async-start | bytes 12582912 | tf_op jit(solution)/shard_map/all_to_all | solution.py:53
  32.6 431.7 %reduce-scatter.2.cloned.1.call-start = ((), (), s32[]{:S(2)}) async-start(), calls=%async_computation.3 | async-start | bytes 8650752 | tf_op jit(solution)/shard_map/reduce_scatter | solution.py:111
  207.8 5.8 %copy-start.1 = (bf16[512,8192]{1,0:T(8,128)(2,1)S(1)}, bf16[512,8192]{1,0:T(8,128)(2,1)}, u32[]{:S(2)}) copy-start(bf16[512,8192]{1,0:T(8,128)(2,1)} %all-gather.2.cloned.1.call-done) | copy-start | bytes 25165828
  223.5 10.4 %collective-permute-start = (bf16[2,2,256,128]{2,3,1,0:T(8,128)(2,1)S(1)}, bf16[2,2,256,128]{2,3,1,0:T(8,128)(2,1)S(1)}, u32[]{:S(2)}, u32[]{:S(2)}) collective-permute-start(bf16[2,2,256,128]{2,3,1,0:T(8,128)(2,1)S(1)} %pad_maximum_fusion.1), channel_id=1, source_target_pairs={{0,1},{1,2},{2,3},{3,4},{4,5},{5,6},{6,7},{8,9},{9,10},{10,11},{11... | collective-permute-start | bytes 786440 | tf_op jit(solution)/shard_map/ppermute | solution.py:13
  233.9 9.5 %collective-permute-start.1 = (bf16[2,2,256,128]{2,3,1,0:T(8,128)(2,1)S(1)}, bf16[2,2,256,128]{2,3,1,0:T(8,128)(2,1)S(1)}, u32[]{:S(2)}, u32[]{:S(2)}) collective-permute-start(bf16[2,2,256,128]{2,3,1,0:T(8,128)(2,1)S(1)} %collective-permute-done), channel_id=1, source_target_pairs={{0,1},{1,2},{2,3},{3,4},{4,5},{5,6},{6,7},{8,9},{9,10},{10,11},{11... | collective-permute-start | bytes 786440 | tf_op jit(solution)/shard_map/ppermute | solution.py:13
  243.5 8.6 %collective-permute-start.2 = (bf16[2,2,256,128]{2,3,1,0:T(8,128)(2,1)S(1)}, bf16[2,2,256,128]{2,3,1,0:T(8,128)(2,1)S(1)}, u32[]{:S(2)}, u32[]{:S(2)}) collective-permute-start(bf16[2,2,256,128]{2,3,1,0:T(8,128)(2,1)S(1)} %collective-permute-done.1), channel_id=1, source_target_pairs={{0,1},{1,2},{2,3},{3,4},{4,5},{5,6},{6,7},{8,9},{9,10},{10,11},{11... | collective-permute-start | bytes 786440 | tf_op jit(solution)/shard_map/ppermute | solution.py:13
  252.1 37.8 %copy-start.3 = (bf16[2,2,256,128]{2,3,1,0:T(8,128)(2,1)}, bf16[2,2,256,128]{2,3,1,0:T(8,128)(2,1)S(1)}, u32[]{:S(2)}) copy-start(bf16[2,2,256,128]{2,3,1,0:T(8,128)(2,1)S(1)} %collective-permute-done.2) | copy-start | bytes 786436
  252.1 8.3 %collective-permute-start.3 = (bf16[2,2,256,128]{2,3,1,0:T(8,128)(2,1)S(1)}, bf16[2,2,256,128]{2,3,1,0:T(8,128)(2,1)S(1)}, u32[]{:S(2)}, u32[]{:S(2)}) collective-permute-start(bf16[2,2,256,128]{2,3,1,0:T(8,128)(2,1)S(1)} %collective-permute-done.2), channel_id=1, source_target_pairs={{0,1},{1,2},{2,3},{3,4},{4,5},{5,6},{6,7},{8,9},{9,10},{10,11},{11... | collective-permute-start | bytes 786440 | tf_op jit(solution)/shard_map/ppermute | solution.py:13
  260.3 8.4 %collective-permute-start.4 = (bf16[2,2,256,128]{2,3,1,0:T(8,128)(2,1)S(1)}, bf16[2,2,256,128]{2,3,1,0:T(8,128)(2,1)S(1)}, u32[]{:S(2)}, u32[]{:S(2)}) collective-permute-start(bf16[2,2,256,128]{2,3,1,0:T(8,128)(2,1)S(1)} %collective-permute-done.3), channel_id=1, source_target_pairs={{0,1},{1,2},{2,3},{3,4},{4,5},{5,6},{6,7},{8,9},{9,10},{10,11},{11... | collective-permute-start | bytes 786440 | tf_op jit(solution)/shard_map/ppermute | solution.py:13
  268.7 9.6 %collective-permute-start.5 = (bf16[2,2,256,128]{2,3,1,0:T(8,128)(2,1)S(1)}, bf16[2,2,256,128]{2,3,1,0:T(8,128)(2,1)S(1)}, u32[]{:S(2)}, u32[]{:S(2)}) collective-permute-start(bf16[2,2,256,128]{2,3,1,0:T(8,128)(2,1)S(1)} %collective-permute-done.4), channel_id=1, source_target_pairs={{0,1},{1,2},{2,3},{3,4},{4,5},{5,6},{6,7},{8,9},{9,10},{10,11},{11... | collective-permute-start | bytes 786440 | tf_op jit(solution)/shard_map/ppermute | solution.py:13
  278.4 10.4 %collective-permute-start.6 = (bf16[2,2,256,128]{2,3,1,0:T(8,128)(2,1)S(1)}, bf16[2,2,256,128]{2,3,1,0:T(8,128)(2,1)S(1)}, u32[]{:S(2)}, u32[]{:S(2)}) collective-permute-start(bf16[2,2,256,128]{2,3,1,0:T(8,128)(2,1)S(1)} %collective-permute-done.5), channel_id=1, source_target_pairs={{0,1},{1,2},{2,3},{3,4},{4,5},{5,6},{6,7},{8,9},{9,10},{10,11},{11... | collective-permute-start | bytes 786440 | tf_op jit(solution)/shard_map/ppermute | solution.py:13
  293.3 172.0 %copy-start.2 = (bf16[256,256]{1,0:T(8,128)(2,1)S(1)}, bf16[256,256]{1,0:T(8,128)(2,1)}, u32[]{:S(2)}) copy-start(bf16[256,256]{1,0:T(8,128)(2,1)} %param.8) | copy-start | bytes 393220
Sparse Core Ops, SparseCore 0:
  12.6 195.1 all-gather.1
  299.0 165.2 reduce-scatter.1
where the time goes:
time: 474 us; the launch traced here: 473 us
  waiting for transfers between devices  365 us (77%)
  starting transfers between devices  41.4 us (9%)
  matrix products  20.8 us (4%)
  local copies, waits for them, and re-layouts  18.6 us (4%)
  other arithmetic  13.8 us (3%)
  between operations  13.8 us (3%)
    reduce_scatter x1, waiting for transfers between devices, shards(): lax.psum_scatter(lax.dot_general(out_weight, attn_flat, (((0,), (1,)), ((...  165 us
    all_to_all x1, waiting for transfers between devices, shards(): lax.all_to_all(qkv_weight, 'fsdp', split_axis=1, concat_axis=0, tiled=True)  161 us
    ppermute x7, waiting for transfers between devices, from_behind(): return lax.ppermute(block, axis, route)  32.7 us
    ppermute x7, starting transfers between devices, from_behind(): return lax.ppermute(block, axis, route)  29.8 us
    all_to_all x1, starting transfers between devices, shards(): lax.all_to_all(qkv_weight, 'fsdp', split_axis=1, concat_axis=0, tiled=True)  11.6 us
  transfers between devices with their start and end apart: 10, of which 10 were waited for; matrix products, arithmetic and copies ran while one was open for 4% of the time, Pallas kernels for 0%

commit v1 on v0

--- a/solution.py
+++ b/solution.py
@@ -50,7 +50,12 @@
     var_rows = (picked_rows + change).astype(jnp.bfloat16)
     placed_rows = jnp.dot(placer, var_rows, preferred_element_type=jnp.float32).astype(jnp.bfloat16)
     variant = jnp.where(changed[:, None], placed_rows, hidden)
-    head_w = lax.all_to_all(qkv_weight, "fsdp", split_axis=1, concat_axis=0, tiled=True)
+    head_w = jnp.concatenate(
+        lax.all_to_all(
+            jnp.stack(jnp.split(qkv_weight, lax.axis_size("fsdp"), axis=1)), "fsdp", 0, 0
+        ),
+        axis=0,
+    )
     block_pos = my_block * tok_rows + jnp.arange(tok_rows)
 
     def finish(proj_rows, positions):

time: 474 us -> 488 us (1.030)
  local copies, waits for them, and re-layouts: 18.6 us -> 52 us
  waiting for transfers between devices: 365 us -> 352 us
  starting transfers between devices: 41.4 us -> 33.9 us
    all_to_all x1, waiting for transfers between devices: 161 us -> 34.6 us  [shards(): lax.all_to_all(jnp.stack(jnp.split(qkv_weight, lax.axis_size('fsdp'), axi...]
    all_gather x1, waiting for transfers between devices: 5.24 us -> 117 us  [shards(): lax.all_gather(dense_rows, 'fsdp', axis=1, tiled=True).astype(jnp.float32)]
    unnamed x11 -> x37, local copies, waits for them, and re-layouts: 9.09 us -> 50.4 us
    all_to_all x1 -> x0, local copies, waits for them, and re-layouts: 8.64 us -> none  [shards(): lax.all_to_all(qkv_weight, 'fsdp', split_axis=1, concat_axis=0, tiled=True)]
    ppermute x7, starting transfers between devices: 29.8 us -> 22.3 us  [from_behind(): return lax.ppermute(block, axis, route)]
    ppermute x7, waiting for transfers between devices: 32.7 us -> 40 us  [from_behind(): return lax.ppermute(block, axis, route)]
    reduce_scatter x1, waiting for transfers between devices: 165 us -> 160 us  [shards(): lax.psum_scatter(lax.dot_general(out_weight, attn_flat, (((0,), (1,)), ((...]
  transfers between devices with their start and end apart: 10 -> 10, of which waited for: 10 -> 10; matrix products, arithmetic and copies ran while one was open for 4% -> 12% of each run, Pallas kernels for 0% -> 0%
where the time goes in v1:
time: 488 us; the launch traced here: 487 us
  waiting for transfers between devices  352 us (72%)
  local copies, waits for them, and re-layouts  52 us (11%)
  starting transfers between devices  33.9 us (7%)
  matrix products  21.6 us (4%)
  between operations  13.8 us (3%)
  other arithmetic  13.6 us (3%)
    reduce_scatter x1, waiting for transfers between devices, shards(): lax.psum_scatter(lax.dot_general(out_weight, attn_flat, (((0,), (1,)), ((...  160 us
    all_gather x1, waiting for transfers between devices, shards(): lax.all_gather(dense_rows, 'fsdp', axis=1, tiled=True).astype(jnp.float32)  117 us
    unnamed x37, local copies, waits for them, and re-layouts  50.4 us
    ppermute x7, waiting for transfers between devices, from_behind(): return lax.ppermute(block, axis, route)  40 us
    all_to_all x1, waiting for transfers between devices, shards(): lax.all_to_all(jnp.stack(jnp.split(qkv_weight, lax.axis_size('fsdp'), axi...  34.6 us
    ppermute x7, starting transfers between devices, from_behind(): return lax.ppermute(block, axis, route)  22.3 us
    all_to_all x1, starting transfers between devices, shards(): lax.all_to_all(jnp.stack(jnp.split(qkv_weight, lax.axis_size('fsdp'), axi...  11.6 us
  transfers between devices with their start and end apart: 10, of which 10 were waited for; matrix products, arithmetic and copies ran while one was open for 12% of the time, Pallas kernels for 0%

profile of v1, /device:TPU:8, one launch (start us, length us, event | category | flops | bytes accessed | tf_op | source)
XLA Modules:
  0.0 486.6 jit_solution(11250850453023393324)
XLA Ops:
  12.5 1.6 bitcast_dynamic-update-slice_fusion.31
  28.7 1.7 bitcast_dynamic-update-slice_fusion.21
  62.8 1.6 bitcast_dynamic-update-slice_fusion
  64.5 11.6 %all-to-all-start = ((bf16[32,256,384]{2,1,0:T(8,128)(2,1)}), bf16[32,256,384]{2,1,0:T(8,128)(2,1)}, u32[]{:S(2)}, u32[]{:S(2)}) async-start(bf16[32,256,384]{2,1,0:T(8,128)(2,1)} %bitcast_dynamic-update-slice_fusion), calls=%async_computation | async-start | bytes 12582912 | tf_op jit(solution)/shard_map/all_to_all | solution.py:54
  76.2 117.0 %all-gather.2.cloned.1.call-done = bf16[512,8192]{1,0:T(8,128)(2,1)} async-done(((bf16[512,256]{1,0:T(8,128)(2,1)}), bf16[512,8192]{1,0:T(8,128)(2,1)}) %all-gather.2.cloned.1.call-update) | async-done | bytes 8388624 | tf_op jit(solution)/shard_map/all_gather | solution.py:70
  193.1 5.1 %fusion.1 = f32[512]{0:T(512)S(1)} fusion(bf16[512,8192]{1,0:T(8,128)(2,1)} %all-gather.2.cloned.1.call-done), kind=kLoop, calls=%fused_computation.3 | loop fusion | flops 12582400 | bytes 8390656 | tf_op jit(solution)/shard_map/reduce_sum | solution.py:73
  198.2 34.6 %all-to-all-done = bf16[32,256,384]{2,1,0:T(8,128)(2,1)} async-done(((bf16[32,256,384]{2,1,0:T(8,128)(2,1)}), bf16[32,256,384]{2,1,0:T(8,128)(2,1)}, u32[]{:S(2)}, u32[]{:S(2)}) %all-to-all-start) | async-done | bytes 6291488 | tf_op jit(solution)/shard_map/all_to_all | solution.py:54
  232.9 8.8 %fusion.113 = (bf16[512,384]{0,1:T(8,128)(2,1)S(1)}, f32[512,384]{0,1:T(8,128)S(1)}) fusion(f32[512]{0:T(512)S(1)} %add_rsqrt_fusion, bf16[8192,384]{1,0:T(8,128)(2,1)} %bitcast.34, bf16[512,8192]{1,0:T(8,128)(2,1)} %all-gather.2.cloned.1.call-done, f32[8192]{0:T(1024)S(1)} %convert_element_type.105), kind=kOutput, calls=%fused_computation.232 | convolution fusion | flops 3234201600 | bytes 15894528 | tf_op jit(solution)/shard_map/dot_general | solution.py:72
  243.7 3.4 collective-permute-start
  247.1 4.9 %collective-permute-done = bf16[2,2,256,128]{2,3,1,0:T(8,128)(2,1)S(1)} collective-permute-done((bf16[2,2,256,128]{2,3,1,0:T(8,128)(2,1)S(1)}, bf16[2,2,256,128]{2,3,1,0:T(8,128)(2,1)S(1)}, u32[]{:S(2)}, u32[]{:S(2)}) %collective-permute-start) | collective-permute-done | bytes 262176 | tf_op jit(solution)/shard_map/ppermute | solution.py:13
  252.0 3.5 collective-permute-start.1
  255.5 4.7 collective-permute-done.1
  260.2 3.5 collective-permute-start.2
  263.8 5.5 %collective-permute-done.2 = bf16[2,2,256,128]{2,3,1,0:T(8,128)(2,1)S(1)} collective-permute-done((bf16[2,2,256,128]{2,3,1,0:T(8,128)(2,1)S(1)}, bf16[2,2,256,128]{2,3,1,0:T(8,128)(2,1)S(1)}, u32[]{:S(2)}, u32[]{:S(2)}) %collective-permute-start.2) | collective-permute-done | bytes 262176 | tf_op jit(solution)/shard_map/ppermute | solution.py:13
  269.3 3.1 collective-permute-start.3
  273.2 6.3 %collective-permute-done.3 = bf16[2,2,256,128]{2,3,1,0:T(8,128)(2,1)S(1)} collective-permute-done((bf16[2,2,256,128]{2,3,1,0:T(8,128)(2,1)S(1)}, bf16[2,2,256,128]{2,3,1,0:T(8,128)(2,1)S(1)}, u32[]{:S(2)}, u32[]{:S(2)}) %collective-permute-start.3) | collective-permute-done | bytes 262176 | tf_op jit(solution)/shard_map/ppermute | solution.py:13
  279.5 2.0 collective-permute-start.4
  282.1 8.2 %collective-permute-done.4 = bf16[2,2,256,128]{2,3,1,0:T(8,128)(2,1)S(1)} collective-permute-done((bf16[2,2,256,128]{2,3,1,0:T(8,128)(2,1)S(1)}, bf16[2,2,256,128]{2,3,1,0:T(8,128)(2,1)S(1)}, u32[]{:S(2)}, u32[]{:S(2)}) %collective-permute-start.4) | collective-permute-done | bytes 262176 | tf_op jit(solution)/shard_map/ppermute | solution.py:13
  290.3 2.0 collective-permute-start.5
  292.8 7.3 %collective-permute-done.5 = bf16[2,2,256,128]{2,3,1,0:T(8,128)(2,1)S(1)} collective-permute-done((bf16[2,2,256,128]{2,3,1,0:T(8,128)(2,1)S(1)}, bf16[2,2,256,128]{2,3,1,0:T(8,128)(2,1)S(1)}, u32[]{:S(2)}, u32[]{:S(2)}) %collective-permute-start.5) | collective-permute-done | bytes 262176 | tf_op jit(solution)/shard_map/ppermute | solution.py:13
  300.2 4.8 collective-permute-start.6
  305.6 3.1 collective-permute-done.6
  312.3 5.6 %fusion.2 = bf16[8192,512]{0,1:T(8,128)(2,1)} fusion(bf16[512,128]{1,0:T(8,128)(2,1)S(1)} %bitcast.173, bf16[128,8192]{1,0:T(8,128)(2,1)S(1)} %copy-done), kind=kOutput, calls=%fused_computation.5 | convolution fusion | flops 1077936128 | bytes 10616832 | tf_op jit(solution)/shard_map/dot_general | solution.py:117
  317.9 160.1 %reduce-scatter.2.cloned.1.call-done = bf16[256,512]{0,1:T(8,128)(2,1)} async-done(((bf16[8192,512]{0,1:T(8,128)(2,1)}), bf16[256,512]{0,1:T(8,128)(2,1)}) %reduce-scatter.2.cloned.1.call-update) | async-done | bytes 262160 | tf_op jit(solution)/shard_map/reduce_scatter | solution.py:116
  (97 shorter events, 62.9 us)
Async XLA Ops:
  6.5 305.8 %copy-start = (bf16[128,8192]{1,0:T(8,128)(2,1)S(1)}, bf16[128,8192]{1,0:T(8,128)(2,1)}, u32[]{:S(2)}) copy-start(bf16[128,8192]{1,0:T(8,128)(2,1)} %param.12) | copy-start | bytes 6291460
  6.5 186.6 %all-gather.2.cloned.1.call-start = ((), (), s32[]{:S(2)}) async-start(), calls=%async_computation.2 | async-start | bytes 8650752 | tf_op jit(solution)/shard_map/all_gather | solution.py:70
  64.5 11.6 %copy-start.2 = (bf16[8192]{0:T(1024)(128)(2,1)S(1)}, bf16[8192]{0:T(1024)(128)(2,1)}, u32[]{:S(2)}) copy-start(bf16[8192]{0:T(1024)(128)(2,1)} %param.9) | copy-start | bytes 49156
  64.5 168.4 %all-to-all-start = ((bf16[32,256,384]{2,1,0:T(8,128)(2,1)}), bf16[32,256,384]{2,1,0:T(8,128)(2,1)}, u32[]{:S(2)}, u32[]{:S(2)}) async-start(bf16[32,256,384]{2,1,0:T(8,128)(2,1)} %bitcast_dynamic-update-slice_fusion), calls=%async_computation | async-start | bytes 12582912 | tf_op jit(solution)/shard_map/all_to_all | solution.py:54
  76.1 402.0 %reduce-scatter.2.cloned.1.call-start = ((), (), s32[]{:S(2)}) async-start(), calls=%async_computation.3 | async-start | bytes 8650752 | tf_op jit(solution)/shard_map/reduce_scatter | solution.py:116
  243.7 8.3 %collective-permute-start = (bf16[2,2,256,128]{2,3,1,0:T(8,128)(2,1)S(1)}, bf16[2,2,256,128]{2,3,1,0:T(8,128)(2,1)S(1)}, u32[]{:S(2)}, u32[]{:S(2)}) collective-permute-start(bf16[2,2,256,128]{2,3,1,0:T(8,128)(2,1)S(1)} %pad_maximum_fusion.1), channel_id=1, source_target_pairs={{0,1},{1,2},{2,3},{3,4},{4,5},{5,6},{6,7},{8,9},{9,10},{10,11},{11... | collective-permute-start | bytes 786440 | tf_op jit(solution)/shard_map/ppermute | solution.py:13
  252.0 8.3 %collective-permute-start.1 = (bf16[2,2,256,128]{2,3,1,0:T(8,128)(2,1)S(1)}, bf16[2,2,256,128]{2,3,1,0:T(8,128)(2,1)S(1)}, u32[]{:S(2)}, u32[]{:S(2)}) collective-permute-start(bf16[2,2,256,128]{2,3,1,0:T(8,128)(2,1)S(1)} %collective-permute-done), channel_id=1, source_target_pairs={{0,1},{1,2},{2,3},{3,4},{4,5},{5,6},{6,7},{8,9},{9,10},{10,11},{11... | collective-permute-start | bytes 786440 | tf_op jit(solution)/shard_map/ppermute | solution.py:13
  260.2 9.0 %collective-permute-start.2 = (bf16[2,2,256,128]{2,3,1,0:T(8,128)(2,1)S(1)}, bf16[2,2,256,128]{2,3,1,0:T(8,128)(2,1)S(1)}, u32[]{:S(2)}, u32[]{:S(2)}) collective-permute-start(bf16[2,2,256,128]{2,3,1,0:T(8,128)(2,1)S(1)} %collective-permute-done.1), channel_id=1, source_target_pairs={{0,1},{1,2},{2,3},{3,4},{4,5},{5,6},{6,7},{8,9},{9,10},{10,11},{11... | collective-permute-start | bytes 786440 | tf_op jit(solution)/shard_map/ppermute | solution.py:13
  269.3 10.2 %collective-permute-start.3 = (bf16[2,2,256,128]{2,3,1,0:T(8,128)(2,1)S(1)}, bf16[2,2,256,128]{2,3,1,0:T(8,128)(2,1)S(1)}, u32[]{:S(2)}, u32[]{:S(2)}) collective-permute-start(bf16[2,2,256,128]{2,3,1,0:T(8,128)(2,1)S(1)} %collective-permute-done.2), channel_id=1, source_target_pairs={{0,1},{1,2},{2,3},{3,4},{4,5},{5,6},{6,7},{8,9},{9,10},{10,11},{11... | collective-permute-start | bytes 786440 | tf_op jit(solution)/shard_map/ppermute | solution.py:13
  279.5 10.8 %collective-permute-start.4 = (bf16[2,2,256,128]{2,3,1,0:T(8,128)(2,1)S(1)}, bf16[2,2,256,128]{2,3,1,0:T(8,128)(2,1)S(1)}, u32[]{:S(2)}, u32[]{:S(2)}) collective-permute-start(bf16[2,2,256,128]{2,3,1,0:T(8,128)(2,1)S(1)} %collective-permute-done.3), channel_id=1, source_target_pairs={{0,1},{1,2},{2,3},{3,4},{4,5},{5,6},{6,7},{8,9},{9,10},{10,11},{11... | collective-permute-start | bytes 786440 | tf_op jit(solution)/shard_map/ppermute | solution.py:13
  290.3 9.9 %collective-permute-start.5 = (bf16[2,2,256,128]{2,3,1,0:T(8,128)(2,1)S(1)}, bf16[2,2,256,128]{2,3,1,0:T(8,128)(2,1)S(1)}, u32[]{:S(2)}, u32[]{:S(2)}) collective-permute-start(bf16[2,2,256,128]{2,3,1,0:T(8,128)(2,1)S(1)} %collective-permute-done.4), channel_id=1, source_target_pairs={{0,1},{1,2},{2,3},{3,4},{4,5},{5,6},{6,7},{8,9},{9,10},{10,11},{11... | collective-permute-start | bytes 786440 | tf_op jit(solution)/shard_map/ppermute | solution.py:13
  300.2 8.5 %collective-permute-start.6 = (bf16[2,2,256,128]{2,3,1,0:T(8,128)(2,1)S(1)}, bf16[2,2,256,128]{2,3,1,0:T(8,128)(2,1)S(1)}, u32[]{:S(2)}, u32[]{:S(2)}) collective-permute-start(bf16[2,2,256,128]{2,3,1,0:T(8,128)(2,1)S(1)} %collective-permute-done.5), channel_id=1, source_target_pairs={{0,1},{1,2},{2,3},{3,4},{4,5},{5,6},{6,7},{8,9},{9,10},{10,11},{11... | collective-permute-start | bytes 786440 | tf_op jit(solution)/shard_map/ppermute | solution.py:13
  317.9 161.1 %copy-start.1 = (bf16[256,256]{1,0:T(8,128)(2,1)S(1)}, bf16[256,256]{1,0:T(8,128)(2,1)}, u32[]{:S(2)}) copy-start(bf16[256,256]{1,0:T(8,128)(2,1)} %param.8) | copy-start | bytes 393220
Sparse Core Ops, SparseCore 0:
  12.6 180.5 all-gather.1
  318.0 159.9 reduce-scatter.1
